TPU v7x, 128 devices: a whole 4x4x4 slice. The times are simulated.
128 devices in a mesh: group: 2 (over y_lo), row: 8 (over x, y_hi), head: 8 (over z, core).
Axes of the slice: x: 4, y: 4 (y_hi: 2, y_lo: 2; y = y_hi * 2 + y_lo), z: 4, core: 2. Of those that a mesh axis runs over, the one named last changes fastest.
Arguments:
- latent: bfloat16 [2048, 3072], P('row', 'head'), may hold values from -6 to 6
- hint: bfloat16 [2048, 3072], P('row', 'head'), may hold values from -6 to 6
- timestep: int32 [1], replicated, may hold values from 0 to 7
- modulation: float32 [2, 8, 3, 3072], P('group'), may hold values from -3 to 3
- qkv_weight: bfloat16 [2, 3, 3072, 3072], P('group', None, None, 'head'), may hold values from -0.109375 to 0.109375
- out_weight: bfloat16 [2, 3072, 3072], P('group', None, 'head'), may hold values from -0.109375 to 0.109375
- zero_weight: bfloat16 [3072, 3072], P(None, 'head'), may hold values from -0.109375 to 0.109375
- cotangent: bfloat16 [2048, 3072], P('row', 'head'), may hold values from -6 to 6
Outputs:
- mixed: bfloat16 [2048, 3072], P('row', 'head')
- latent_grad: float32 [8, 2, 128, 3072], P('row', 'group', None, 'head')
- hint_grad: float32 [8, 2, 128, 3072], P('row', 'group', None, 'head')
- qkv_grad: float32 [3072, 3, 3072], P(('group', 'row'), None, 'head')
- out_grad: float32 [3072, 3072], P(('group', 'row'), 'head')
- zero_grad: float32 [3072, 3072], P(('group', 'row'), 'head')
All inputs are finite; a program needn't handle non-finite values.
Results may differ from a plain program's by a relative error of at most 0.015.
Values may be sent and summed in bfloat16 or wider, within the bound.
No kernel may reach another device: no remote copies, remote signals or barrier semaphores. Data moves between devices by JAX's collectives and lax.ppermute only.
A program may use at most 128 MiB of HBM per device.

v0:
```python
import jax
import jax.numpy as jnp
from jax import lax
from jax.sharding import Mesh
from jax.sharding import PartitionSpec as P

HD = 128
ROW = ("row_0", "row_1")
GROUP_ROW = ("group", "row_0", "row_1")
EPS = 1e-06


def copy_for_each(array, axis):
    copies = jnp.broadcast_to(array, (lax.axis_size(axis), *array.shape))
    return lax.all_to_all(copies, axis, split_axis=0, concat_axis=0, tiled=True)


def in_order(pieces, dim):
    lengths = list(pieces.shape[1:])
    lengths[dim] *= pieces.shape[0]
    return jnp.moveaxis(pieces, 0, dim).reshape(lengths)


def gather_directly(array, axis, dim):
    pieces = copy_for_each(array, axis)
    return in_order(pieces, dim)


def sent_together(arrays, axis, dim, along):
    both = jnp.concatenate(arrays, axis=along)
    filled, at, finished = (lax.all_gather(both, axis, axis=dim, tiled=True), 0, [])
    for a in arrays:
        finished.append(lax.slice_in_dim(filled, at, at + a.shape[along], axis=along))
        at += a.shape[along]
    return tuple(finished)


def in_blocks(array, dim, peers):
    lengths = array.shape
    pieces = array.reshape(*lengths[:dim], peers, lengths[dim] // peers, *lengths[dim + 1 :])
    return jnp.moveaxis(pieces, dim, 0)


def sum_at_owner(array, axis, dim):
    pieces = in_blocks(array, dim, lax.axis_size(axis))
    arrived = lax.all_to_all(pieces, axis, split_axis=0, concat_axis=0, tiled=True)
    return arrived.sum(axis=0)


def from_partner(block, axis, distance):
    count = lax.axis_size(axis)
    route = []
    for low in range(count):
        high = low | 1 << distance
        if high != low and high < count:
            route += [(low, high), (high, low)]
    return lax.ppermute(block, axis, route)


def taken_together(array, axis):
    everything = copy_for_each(array, axis)
    return jnp.sum(everything, axis=0)


def together(arrays, axis):
    ravelled, at, finished = (jnp.concatenate([a.reshape(-1) for a in arrays]), 0, [])
    subtotal = taken_together(ravelled, axis)
    for a in arrays:
        finished.append(subtotal[at : at + a.size].reshape(a.shape))
        at += a.size
    return tuple(finished)


def sum_in_order(pieces, axes, order):
    lengths = [lax.axis_size(a) for a in axes]
    pieces = pieces.reshape(*lengths, *pieces.shape[1:])
    pieces = pieces.transpose(*order, *range(len(axes), pieces.ndim))
    pieces = pieces.reshape(-1, *pieces.shape[len(axes) :])
    for k in order:
        pieces = lax.psum_scatter(pieces, axes[k], scatter_dimension=0, tiled=True)
    return pieces[0]


def scatter_axes(array, axes, order, dim):
    peers = lax.axis_size(axes)
    return sum_in_order(in_blocks(array, dim, peers), axes, order)


def on_device(latent, hint, timestep, modulation, qkv_weight, out_weight, zero_weight, cotangent):
    tok, width = latent.shape
    heads_dev = width // HD
    scaling = HD ** (-0.5)
    control = lax.axis_index("group") == 0
    ctrl_mask = control.astype(jnp.float32)
    head_pos = lax.axis_index("head")
    steps_count = modulation.shape[1]
    pick = (lax.broadcasted_iota(jnp.int32, (steps_count,), 0) == timestep[0]).astype(jnp.float32)
    mods = jnp.sum(modulation[0] * pick[:, None, None], axis=0)
    shift, scale, gate = (mods[0], mods[1], mods[2])
    gate_dev = lax.dynamic_slice_in_dim(gate, head_pos * width, width, 0)
    scale_dev = lax.dynamic_slice_in_dim(scale, head_pos * width, width, 0)
    summed = (latent.astype(jnp.float32) + hint.astype(jnp.float32)).astype(jnp.bfloat16)
    inputs = jnp.where(control, summed, latent)
    whole = gather_directly(inputs, "head", 1)
    full_width = whole.shape[1]
    whole_f = whole.astype(jnp.float32)
    mean = jnp.mean(whole_f, axis=-1, keepdims=True)
    centred = whole_f - mean
    var = jnp.mean(centred * centred, axis=-1, keepdims=True)
    rstd = lax.rsqrt(var + EPS)
    nhat = centred * rstd
    normed = (nhat * (1.0 + scale) + shift).astype(jnp.bfloat16)
    w_qkv = qkv_weight[0]
    projected_qkv = jnp.einsum(
        "td,pde->pte", normed, w_qkv, preferred_element_type=jnp.float32
    ).astype(jnp.bfloat16)
    query, keys, values = (projected_qkv[0], projected_qkv[1], projected_qkv[2])
    q_heads = query.reshape(tok, heads_dev, HD)
    start_carry = (
        jnp.full((heads_dev, tok), -1e30, jnp.float32),
        jnp.zeros((heads_dev, tok), jnp.float32),
        jnp.zeros((tok, heads_dev, HD), jnp.float32),
    )

    def attend(carry, block):
        peak, total, acc = carry
        k_heads = block[0].reshape(-1, heads_dev, HD)
        v_heads = block[1].reshape(-1, heads_dev, HD)
        scores = (
            jnp.einsum("thd,shd->hts", q_heads, k_heads, preferred_element_type=jnp.float32)
            * scaling
        )
        new_peak = jnp.maximum(peak, jnp.max(scores, axis=-1))
        factor = jnp.exp(peak - new_peak)
        weights = jnp.exp(scores - new_peak[:, :, None])
        total = total * factor + jnp.sum(weights, axis=-1)
        acc = acc * factor.T[:, :, None] + jnp.einsum(
            "hts,shd->thd",
            weights.astype(jnp.bfloat16),
            v_heads,
            preferred_element_type=jnp.float32,
        )
        return ((new_peak, total, acc), None)

    kv_full = sent_together((keys, values), ROW, 0, 1)
    carry = start_carry
    key_rows = kv_full[0]
    rows = key_rows.shape[0]
    count = max(rows // tok, 1)
    size = rows // count
    blocks = (key_rows.reshape(count, size, width), kv_full[1].reshape(count, size, width))
    carry, unused = lax.scan(attend, carry, blocks)
    peak, total, acc = carry
    attn = (acc / total.T[:, :, None]).reshape(tok, width).astype(jnp.bfloat16)
    lse = peak + jnp.log(total)
    w_out = out_weight[0]
    branch_term = lax.dot_general(
        attn, w_out, (((1,), (1,)), ((), ())), preferred_element_type=jnp.float32
    )
    branch = sum_at_owner(branch_term, "head", 1)
    state = (inputs.astype(jnp.float32) + gate_dev * branch).astype(jnp.bfloat16)
    other_state = from_partner(state, "group", 0)
    control_out = jnp.where(control, state, other_state)
    main_out = jnp.where(control, other_state, state)
    hint_term = lax.dot_general(
        control_out, zero_weight, (((1,), (1,)), ((), ())), preferred_element_type=jnp.float32
    )
    projected = sum_at_owner(hint_term, "head", 1)
    mixed = (main_out.astype(jnp.float32) + projected).astype(jnp.bfloat16)
    cot_full = gather_directly(cotangent, "head", 1)
    hint_back = jnp.dot(cot_full, zero_weight, preferred_element_type=jnp.float32).astype(
        jnp.bfloat16
    )
    incoming = jnp.where(control, hint_back, cotangent)
    gated = (gate_dev * incoming.astype(jnp.float32)).astype(jnp.bfloat16)
    gated_full = gather_directly(gated, "head", 1)
    attn_grad = jnp.dot(gated_full, w_out, preferred_element_type=jnp.float32).astype(jnp.bfloat16)
    dsum = jnp.sum(
        (attn_grad.astype(jnp.float32) * attn.astype(jnp.float32)).reshape(tok, heads_dev, HD),
        axis=-1,
    )
    g_heads = attn_grad.reshape(tok, heads_dev, HD)
    full_keys, full_values = kv_full
    block_count = full_keys.shape[0] // tok
    key_blocks = (
        full_keys.reshape(block_count, tok, width),
        full_values.reshape(block_count, tok, width),
    )

    def backward_step(dq_acc, block):
        k_heads = block[0].reshape(tok, heads_dev, HD)
        v_heads = block[1].reshape(tok, heads_dev, HD)
        scores = (
            jnp.einsum("thd,shd->hts", q_heads, k_heads, preferred_element_type=jnp.float32)
            * scaling
        )
        probs = jnp.exp(scores - lse[:, :, None])
        dprobs = jnp.einsum("thd,shd->hts", g_heads, v_heads, preferred_element_type=jnp.float32)
        dscores = (probs * (dprobs - dsum.T[:, :, None])).astype(jnp.bfloat16)
        dq_acc = dq_acc + jnp.einsum(
            "hts,shd->thd", dscores, k_heads, preferred_element_type=jnp.float32
        )
        return (dq_acc, None)

    dq_acc, key_terms = lax.scan(
        backward_step, jnp.zeros((tok, heads_dev, HD), jnp.float32), key_blocks
    )
    dquery = (dq_acc * scaling).reshape(tok, width).astype(jnp.bfloat16)
    gathered = (
        lax.all_gather(query.astype(jnp.float32), ROW, axis=0, tiled=True).astype(query.dtype),
        lax.all_gather(attn_grad.astype(jnp.float32), ROW, axis=0, tiled=True).astype(
            attn_grad.dtype
        ),
        lax.all_gather(lse.T, ROW, axis=0, tiled=True),
        lax.all_gather(dsum, ROW, axis=0, tiled=True),
    )
    query_blocks = (
        gathered[0].reshape(block_count, tok, width),
        gathered[1].reshape(block_count, tok, width),
        gathered[2].reshape(block_count, tok, heads_dev),
        gathered[3].reshape(block_count, tok, heads_dev),
    )
    own_keys = keys.reshape(tok, heads_dev, HD)
    own_values = values.reshape(tok, heads_dev, HD)

    def owner_step(carry, block):
        dk_acc, dv_acc = carry
        qh = block[0].reshape(tok, heads_dev, HD)
        gh = block[1].reshape(tok, heads_dev, HD)
        scores = (
            jnp.einsum("thd,shd->hts", qh, own_keys, preferred_element_type=jnp.float32) * scaling
        )
        probs = jnp.exp(scores - block[2].T[:, :, None])
        dprobs = jnp.einsum("thd,shd->hts", gh, own_values, preferred_element_type=jnp.float32)
        dscores = (probs * (dprobs - block[3].T[:, :, None])).astype(jnp.bfloat16)
        dk_acc = dk_acc + jnp.einsum(
            "hts,thd->shd", dscores, qh, preferred_element_type=jnp.float32
        )
        dv_acc = dv_acc + jnp.einsum(
            "hts,thd->shd", probs.astype(jnp.bfloat16), gh, preferred_element_type=jnp.float32
        )
        return ((dk_acc, dv_acc), None)

    empty = jnp.zeros((tok, heads_dev, HD), jnp.float32)
    (dk_acc, dv_acc), unused = lax.scan(owner_step, (empty, empty), query_blocks)
    dkey_sum = (dk_acc * scaling).reshape(tok, width)
    dval_sum = dv_acc.reshape(tok, width)
    grads = jnp.stack([dquery, dkey_sum.astype(jnp.bfloat16), dval_sum.astype(jnp.bfloat16)])
    norm_term = jnp.einsum("pte,pde->td", grads, w_qkv, preferred_element_type=jnp.float32)
    nhat_dev = lax.dynamic_slice_in_dim(nhat, head_pos * width, width, 1)
    dnorm = sum_at_owner(norm_term, "head", 1)
    scaled = dnorm * (1.0 + scale_dev)
    first, second = together(
        (jnp.sum(scaled, axis=-1), jnp.sum(scaled * nhat_dev, axis=-1)), "head"
    )
    first = first[:, None] / full_width
    second = second[:, None] / full_width
    d_in = incoming.astype(jnp.float32) + rstd * (scaled - first - nhat_dev * second)
    half = tok // 2
    group_pos = lax.axis_index("group")
    own_half = lax.dynamic_slice_in_dim(d_in, group_pos * half, half, 0)
    sent_half = lax.dynamic_slice_in_dim(d_in, (1 - group_pos) * half, half, 0)
    other_half = from_partner(sent_half, "group", 0)
    latent_grad = (own_half + other_half)[None, None]
    hint_grad = jnp.where(control, own_half, other_half)[None, None]
    offset = group_pos * half
    cot_half = lax.dynamic_slice_in_dim(cot_full, offset, half, 0)
    control_half = lax.dynamic_slice_in_dim(control_out, offset, half, 0)
    columns = normed
    qkv_grad = scatter_axes(
        jnp.einsum("tc,pte->cpe", columns, grads, preferred_element_type=jnp.float32) * ctrl_mask,
        GROUP_ROW,
        (1, 0, 2),
        0,
    )
    columns = gated_full
    out_grad = lax.psum_scatter(
        lax.dot_general(columns, attn, (((0,), (0,)), ((), ())), preferred_element_type=jnp.float32)
        * ctrl_mask,
        GROUP_ROW,
        scatter_dimension=0,
        tiled=True,
    )
    columns = cot_half
    zero_grad = lax.psum_scatter(
        lax.dot_general(
            columns, control_half, (((0,), (0,)), ((), ())), preferred_element_type=jnp.float32
        ),
        GROUP_ROW,
        scatter_dimension=0,
        tiled=True,
    )
    return (mixed, latent_grad, hint_grad, qkv_grad, out_grad, zero_grad)


def solution(mesh):
    torus = Mesh(
        mesh.devices.reshape(mesh.shape["group"], 4, 2, mesh.shape["head"]),
        ("group", "row_0", "row_1", "head"),
    )
    return jax.shard_map(
        on_device,
        mesh=torus,
        in_specs=(
            P(ROW, "head"),
            P(ROW, "head"),
            P(),
            P("group", None, None, None),
            P("group", None, None, "head"),
            P("group", None, "head"),
            P(None, "head"),
            P(ROW, "head"),
        ),
        out_specs=(
            P(ROW, "head"),
            P(ROW, "group", None, "head"),
            P(ROW, "group", None, "head"),
            P(GROUP_ROW, None, "head"),
            P(GROUP_ROW, "head"),
            P(GROUP_ROW, "head"),
        ),
        check_vma=False,
    )
```

profile of v0, /device:TPU:1, one launch (start us, length us, event | category | flops | bytes accessed | tf_op | source)
XLA Modules:
  0.0 831.2 jit_solution(7527920485716257239)
XLA Ops:
  7.2 1.3 fusion.48
  8.6 1.3 broadcast_in_dim.24
  9.8 6.8 all-to-all-start
  18.1 19.2 %all-to-all-done = bf16[8,256,384]{2,1,0:T(8,128)(2,1)} async-done(((bf16[8,256,384]{2,1,0:T(8,128)(2,1)}), bf16[8,256,384]{2,1,0:T(8,128)(2,1)}, u32[]{:S(2)}, u32[]{:S(2)}) %all-to-all-start) | async-done | bytes 1572896 | tf_op jit(solution)/shard_map/all_to_all | solution.py:15
  37.3 2.6 copy.167
  39.9 1.9 convert_reduce_fusion
  43.4 5.3 fusion.37
  51.1 1.1 copy.171
  52.2 59.9 %all-gather.5.cloned.1.call-done = bf16[2048,768]{1,0:T(8,128)(2,1)} async-done(((bf16[256,768]{1,0:T(8,128)(2,1)}), bf16[2048,768]{1,0:T(8,128)(2,1)}) %all-gather.5.cloned.1.call-update) | async-done | bytes 3145744 | tf_op jit(solution)/shard_map/all_gather | solution.py:31
  112.1 3.9 fusion.59
  116.0 2.6 copy.172
  118.6 2.7 copy.170
  121.2 15.0 %while.39 = (s32[]{:T(128)}, f32[3,256]{1,0:T(4,128)S(1)}, f32[3,256]{1,0:T(4,128)S(1)}, f32[256,3,128]{0,2,1:T(8,128)S(1)}, bf16[8,256,384]{1,2,0:T(8,128)(2,1)...) while((s32[]{:T(128)}, f32[3,256]{1,0:T(4,128)S(1)}, ...), condition=%wide.region_6.7_spmd.clone, body=%wide.region_3.6_spmd.clone.sunk | while | flops 102142464 | bytes 4571253 | solution.py:152
  137.0 2.7 convolution_bitcast_fusion.2
  139.7 6.0 all-to-all-start.1
  145.8 37.4 %all-to-all-done.1 = f32[8,256,384]{2,1,0:T(8,128)} async-done(((f32[8,256,384]{2,1,0:T(8,128)}), f32[8,256,384]{2,1,0:T(8,128)}, u32[]{:S(2)}, u32[]{:S(2)}) %all-to-all-start.1) | async-done | bytes 3145760 | tf_op jit(solution)/shard_map/all_to_all | solution.py:46
  183.2 1.3 broadcast_in_dim.25
  184.5 5.1 all-to-all-start.3
  190.4 1.3 fusion.52
  191.7 2.1 reduce_sum.102
  193.7 16.6 %all-to-all-done.3 = bf16[8,256,384]{1,2,0:T(8,128)(2,1)} async-done(((bf16[8,256,384]{1,2,0:T(8,128)(2,1)}), bf16[8,256,384]{1,2,0:T(8,128)(2,1)}, u32[]{:S(2)}, u32[]{:S(2)}) %all-to-all-start.3) | async-done | bytes 1572896 | tf_op jit(solution)/shard_map/all_to_all | solution.py:15
  210.4 4.0 multiply_convert_fusion.2
  215.5 1.3 broadcast_in_dim.26
  216.7 5.1 all-to-all-start.4
  221.8 3.5 convert_element_type.155
  226.1 1.1 copy.189
  227.2 1.7 copy.184
  229.0 1.7 copy.187
  230.7 3.6 copy.210
  234.3 4.2 subtract_multiply_fusion
  238.5 1.7 copy.178
  240.3 29.6 %all_gather.17 = f32[2048,3]{0,1:T(4,128)} all-gather(f32[256,3]{0,1:T(4,128)S(1)} %bitcast.246), channel_id=1, replica_groups=mesh['group'=2,'row_0'=4,'row_1'=2,'head'=8] {'row_0','row_1'}, dimensions={0}, use_global_device_ids=true | all-gather | bytes 27648 | tf_op jit(solution)/shard_map/all_gather | solution.py:214
  269.9 3.3 convert_multiply_fusion
  273.2 1.2 copy.179
  275.7 15.6 %while.40 = (s32[]{:T(128)}, f32[256,3,128]{0,2,1:T(8,128)S(1)}, bf16[8,256,384]{1,2,0:T(8,128)(2,1)}, bf16[256,3,128]{2,0,1:T(8,128)(2,1)S(1)}, f32[3,256]{1,0:...) while((s32[]{:T(128)}, f32[256,3,128]{0,2,1:T(8,128)S(1)}, ...), condition=%wide.region_11.12_spmd.clone, body=%wide.region_10.11_spmd.clone.sunk | while | flops 152174592 | bytes 4135035 | solution.py:205
  275.7 1.1 constant_dynamic-slice_fusion.13
  289.4 1.1 constant_dynamic-slice_fusion.13
  291.6 28.0 %all_gather.19 = f32[2048,3]{0,1:T(4,128)S(1)} all-gather(f32[256,3]{0,1:T(4,128)S(1)} %get-tuple-element.758), channel_id=1, replica_groups=mesh['group'=2,'row_0'=4,'row_1'=2,'head'=8] {'row_0','row_1'}, dimensions={0}, use_global_device_ids=true | all-gather | bytes 27648 | tf_op jit(solution)/shard_map/all_gather | solution.py:215
  319.6 10.1 %all-gather.7.cloned.1.call-done = bf16[2048,384]{1,0:T(8,128)(2,1)} async-done(((bf16[256,384]{1,0:T(8,128)(2,1)}), bf16[2048,384]{1,0:T(8,128)(2,1)}) %all-gather.7.cloned.1.call-update) | async-done | bytes 1572880 | tf_op jit(solution)/shard_map/all_gather | solution.py:211
  329.7 25.7 %while.41 = (s32[]{:T(128)}, f32[256,3,128]{0,2,1:T(8,128)S(1)}, f32[256,3,128]{0,2,1:T(8,128)S(1)}, bf16[8,256,384]{2,1,0:T(8,128)(2,1)}, bf16[256,3,128]{2,0,1...) while((s32[]{:T(128)}, f32[256,3,128]{0,2,1:T(8,128)S(1)}, ...), condition=%wide.region_13.14_spmd.clone, body=%wide.region_12.13_spmd.clone.sunk | while | flops 202899456 | bytes 6703240 | solution.py:245
  355.9 9.3 %broadcast_multiply_fusion = f32[3072,3,384]{2,0,1:T(8,128)} fusion(f32[]{:T(128)S(6)} %convert_element_type.185, f32[256,3072]{1,0:T(8,128)} %subtract_multiply_fusion, f32[3072]{0:T(1024)S(1)} %bitcast.251, f32[3072]{0:T(1024)S(1)} %bitcast.250, bf16[1,256,384]{2,1,0:T(8,128)(2,1)S(1)} %copy.192, bf16[1,256,384]{2,1,0:T(8,128)(2,1)S(1)} %copy.191, ...), kind=kOutput, calls=%fused_computation.47 | convolution fusion | flops 1819607040 | bytes 17915908 | tf_op jit(solution)/shard_map/tc,pte->cpe/dot_general | solution.py:271
  365.1 11.7 %copy.197 = f32[4,2,2,192,3,384]{5,3,4,2,1,0:T(8,128)} copy(f32[4,2,2,192,3,384]{5,3,2,0,1,4:T(8,128)} %bitcast.215) | data formatting | bytes 28311552 | tf_op jit(solution)/shard_map/transpose | solution.py:77
  376.9 127.9 %reduce-scatter.6.cloned.1.call-done = f32[4,192,3,384]{3,1,2,0:T(8,128)} async-done(((f32[16,192,3,384]{3,1,2,0:T(8,128)}), f32[4,192,3,384]{3,1,2,0:T(8,128)}) %reduce-scatter.6.cloned.1.call-update) | async-done | bytes 3538960 | tf_op jit(solution)/shard_map/reduce_scatter | solution.py:80
  504.9 1.3 collective-permute-start
  506.2 4.5 collective-permute-done
  510.7 4.1 fusion.45
  515.8 5.0 convolution_multiply_fusion.3
  520.8 6.9 convolution_bitcast_fusion.3
  527.7 6.0 all-to-all-start.5
  534.7 1.8 copy.219
  536.5 34.7 %all-to-all-done.5 = f32[8,256,384]{2,1,0:T(8,128)} async-done(((f32[8,256,384]{2,1,0:T(8,128)}), f32[8,256,384]{2,1,0:T(8,128)}, u32[]{:S(2)}, u32[]{:S(2)}) %all-to-all-start.5) | async-done | bytes 3145760 | tf_op jit(solution)/shard_map/all_to_all | solution.py:46
  571.2 5.3 all-to-all-start.2
  577.9 2.1 reduce_sum.105
  580.0 1.2 multiply_reduce_fusion.2
  581.2 32.9 %all-to-all-done.2 = f32[8,256,384]{2,1,0:T(8,128)} async-done(((f32[8,256,384]{2,1,0:T(8,128)}), f32[8,256,384]{2,1,0:T(8,128)}, u32[]{:S(2)}, u32[]{:S(2)}) %all-to-all-start.2) | async-done | bytes 3145760 | tf_op jit(solution)/shard_map/all_to_all | solution.py:46
  614.7 4.2 all-to-all-start.6
  618.9 2.3 reduce_sum.103
  621.2 2.8 all-to-all-done.6
  625.3 1.3 multiply_add_fusion
  626.7 1.3 collective-permute-start.1
  628.7 13.9 %collective-permute-done.1 = f32[128,384]{1,0:T(8,128)S(1)} collective-permute-done((f32[128,384]{1,0:T(8,128)S(1)}, f32[128,384]{1,0:T(8,128)S(1)}, u32[]{:S(2)}, u32[]{:S(2)}) %collective-permute-start.1) | collective-permute-done | bytes 196640 | tf_op jit(solution)/shard_map/ppermute | solution.py:57
  643.4 26.1 %reduce-scatter.14.cloned.1.call-done = f32[192,384]{1,0:T(8,128)} async-done(((f32[3072,384]{1,0:T(8,128)}), f32[192,384]{1,0:T(8,128)}) %reduce-scatter.14.cloned.1.call-update) | async-done | bytes 294928 | tf_op jit(solution)/shard_map/reduce_scatter | solution.py:285
  669.5 114.8 %reduce-scatter.12.cloned.1.call-done = f32[192,384]{1,0:T(8,128)} async-done(((f32[3072,384]{1,0:T(8,128)}), f32[192,384]{1,0:T(8,128)}) %reduce-scatter.12.cloned.1.call-update) | async-done | bytes 294928 | tf_op jit(solution)/shard_map/reduce_scatter | solution.py:277
  784.3 40.0 %reduce-scatter.10.cloned.1.call-done = f32[1,192,3,384]{3,1,2,0:T(8,128)} async-done(((f32[2,192,3,384]{3,1,2,0:T(8,128)}), f32[1,192,3,384]{3,1,2,0:T(8,128)}) %reduce-scatter.10.cloned.1.call-update) | async-done | bytes 884752 | tf_op jit(solution)/shard_map/reduce_scatter | solution.py:80
  (231 shorter events, 70.4 us)
Async XLA Ops:
  7.2 129.2 %copy-start = (bf16[1,3072,384]{2,1,0:T(8,128)(2,1)S(1)}, bf16[1,3072,384]{2,1,0:T(8,128)(2,1)}, u32[]{:S(2)}) copy-start(bf16[1,3072,384]{2,1,0:T(8,128)(2,1)} %param.19) | copy-start | bytes 7077892
  8.5 8.8 %copy-start.12 = (f32[1,8,3,3072]{3,1,2,0:T(8,128)S(1)}, f32[1,8,3,3072]{3,1,2,0:T(8,128)}, u32[]{:S(2)}) copy-start(f32[1,8,3,3072]{3,1,2,0:T(8,128)} %param.17) | copy-start | bytes 884740
  9.8 27.5 %all-to-all-start = ((bf16[8,256,384]{2,1,0:T(8,128)(2,1)}), bf16[8,256,384]{2,1,0:T(8,128)(2,1)}, u32[]{:S(2)}, u32[]{:S(2)}) async-start(bf16[8,256,384]{2,1,0:T(8,128)(2,1)} %broadcast_in_dim.24), calls=%async_computation | async-start | bytes 3145728 | tf_op jit(solution)/shard_map/all_to_all | solution.py:15
  16.6 95.5 %all-gather.5.cloned.1.call-start = ((), (), s32[]{:S(2)}) async-start(), calls=%async_computation.12 | async-start | bytes 3538944 | tf_op jit(solution)/shard_map/all_gather | solution.py:31
  39.9 2.0 copy-start.2
  42.4 192.0 %copy-start.17 = (f32[256]{0:T(256)}, f32[256]{0:T(256)S(1)}, u32[]{:S(2)}) copy-start(f32[256]{0:T(256)S(1)} %add_rsqrt_fusion) | copy-start | bytes 3076
  49.4 66.6 %copy-start.8 = (bf16[1,256,384]{2,1,0:T(8,128)(2,1)}, bf16[1,256,384]{2,1,0:T(8,128)(2,1)S(1)}, u32[]{:S(2)}) copy-start(bf16[1,256,384]{2,1,0:T(8,128)(2,1)S(1)} %get-tuple-element.437) | copy-start | bytes 589828
  136.3 0.7 copy-start.5
  139.7 6.0 copy-start.13
  139.7 43.5 %all-to-all-start.1 = ((f32[8,256,384]{2,1,0:T(8,128)}), f32[8,256,384]{2,1,0:T(8,128)}, u32[]{:S(2)}, u32[]{:S(2)}) async-start(f32[8,256,384]{2,1,0:T(8,128)} %convolution_bitcast_fusion.2), calls=%async_computation.1 | async-start | bytes 6291456 | tf_op jit(solution)/shard_map/all_to_all | solution.py:46
  184.5 25.9 %all-to-all-start.3 = ((bf16[8,256,384]{1,2,0:T(8,128)(2,1)}), bf16[8,256,384]{1,2,0:T(8,128)(2,1)}, u32[]{:S(2)}, u32[]{:S(2)}) async-start(bf16[8,256,384]{1,2,0:T(8,128)(2,1)} %broadcast_in_dim.25), calls=%async_computation.3 | async-start | bytes 3145728 | tf_op jit(solution)/shard_map/all_to_all | solution.py:15
  189.6 129.9 %all-gather.9.cloned.1.call-start = ((), (), s32[]{:S(2)}) async-start(), calls=%async_computation.19 | async-start | bytes 1769472 | tf_op jit(solution)/shard_map/all_gather | solution.py:210
  216.7 53.2 %all-to-all-start.4 = ((bf16[8,256,384]{1,2,0:T(8,128)(2,1)}), bf16[8,256,384]{1,2,0:T(8,128)(2,1)}, u32[]{:S(2)}, u32[]{:S(2)}) async-start(bf16[8,256,384]{1,2,0:T(8,128)(2,1)} %broadcast_in_dim.26), calls=%async_computation.4 | async-start | bytes 3145728 | tf_op jit(solution)/shard_map/all_to_all | solution.py:15
  221.8 107.8 %all-gather.7.cloned.1.call-start = ((), (), s32[]{:S(2)}) async-start(), calls=%async_computation.13 | async-start | bytes 1769472 | tf_op jit(solution)/shard_map/all_gather | solution.py:211
  275.5 229.3 %reduce-scatter.6.cloned.1.call-start = ((), (), s32[]{:S(2)}) async-start(), calls=%async_computation.14 | async-start | bytes 17694720 | tf_op jit(solution)/shard_map/reduce_scatter | solution.py:80
  275.7 54.0 %copy-start.3 = (f32[256,3,128]{0,2,1:T(8,128)S(1)}, f32[256,3,128]{0,2,1:T(8,128)}, u32[]{:S(2)}) copy-start(f32[256,3,128]{0,2,1:T(8,128)} %custom-call.5) | copy-start | bytes 1179652
  275.7 54.0 %copy-start.4 = (bf16[256,3,128]{2,0,1:T(8,128)(2,1)S(1)}, bf16[256,3,128]{2,0,1:T(8,128)(2,1)}, u32[]{:S(2)}) copy-start(bf16[256,3,128]{2,0,1:T(8,128)(2,1)} %copy.187) | copy-start | bytes 589828
  329.7 26.2 %copy-start.14 = (f32[1,3072]{1,0:T(1,128)S(1)}, f32[1,3072]{1,0:T(1,128)}, u32[]{:S(2)}) copy-start(f32[1,3072]{1,0:T(1,128)} %get-tuple-element.440) | copy-start | bytes 36868
  329.7 26.2 %copy-start.15 = (f32[1,3072]{1,0:T(1,128)S(1)}, f32[1,3072]{1,0:T(1,128)}, u32[]{:S(2)}) copy-start(f32[1,3072]{1,0:T(1,128)} %get-tuple-element.441) | copy-start | bytes 36868
  376.8 128.0 %copy-start.9 = (bf16[256,384]{1,0:T(8,128)(2,1)S(1)}, bf16[256,384]{1,0:T(8,128)(2,1)}, u32[]{:S(2)}) copy-start(bf16[256,384]{1,0:T(8,128)(2,1)} %get-tuple-element.447) | copy-start | bytes 589828
  376.8 199.7 %reduce-scatter.8.cloned.1.call-start = ((), (), s32[]{:S(2)}) async-start(), calls=%async_computation.15 | async-start | bytes 5308416 | tf_op jit(solution)/shard_map/reduce_scatter | solution.py:80
  504.8 164.7 %reduce-scatter.14.cloned.1.call-start = ((), (), s32[]{:S(2)}) async-start(), calls=%async_computation.18 | async-start | bytes 5013504 | tf_op jit(solution)/shard_map/reduce_scatter | solution.py:285
  504.9 5.8 collective-permute-start
  510.7 4.1 copy-start.10
  514.8 1.0 copy-start.6
  514.8 269.5 %reduce-scatter.12.cloned.1.call-start = ((), (), s32[]{:S(2)}) async-start(), calls=%async_computation.17 | async-start | bytes 5013504 | tf_op jit(solution)/shard_map/reduce_scatter | solution.py:277
  527.7 6.0 copy-start.7
  527.7 43.5 %all-to-all-start.5 = ((f32[8,256,384]{2,1,0:T(8,128)}), f32[8,256,384]{2,1,0:T(8,128)}, u32[]{:S(2)}, u32[]{:S(2)}) async-start(f32[8,256,384]{2,1,0:T(8,128)} %convolution_bitcast_fusion.3), calls=%async_computation.5 | async-start | bytes 6291456 | tf_op jit(solution)/shard_map/all_to_all | solution.py:46
  571.2 42.9 %all-to-all-start.2 = ((f32[8,256,384]{2,1,0:T(8,128)}), f32[8,256,384]{2,1,0:T(8,128)}, u32[]{:S(2)}, u32[]{:S(2)}) async-start(f32[8,256,384]{2,1,0:T(8,128)} %bitcast.227), calls=%async_computation.2 | async-start | bytes 6291456 | tf_op jit(solution)/shard_map/all_to_all | solution.py:46
  576.5 247.8 %reduce-scatter.10.cloned.1.call-start = ((), (), s32[]{:S(2)}) async-start(), calls=%async_computation.16 | async-start | bytes 2654208 | tf_op jit(solution)/shard_map/reduce_scatter | solution.py:80
  577.9 41.0 %copy-start.16 = (f32[384]{0:T(512)}, f32[384]{0:T(512)S(1)}, u32[]{:S(2)}) copy-start(f32[384]{0:T(512)S(1)} %fusion.54) | copy-start | bytes 4612
  614.7 9.3 %all-to-all-start.6 = ((f32[8,1,512]{2,1,0:T(1,128)}), f32[8,1,512]{2,1,0:T(1,128)S(1)}, u32[]{:S(2)}, u32[]{:S(2)}) async-start(f32[8,1,512]{2,1,0:T(1,128)} %broadcast_in_dim.27), calls=%async_computation.6 | async-start | bytes 32768 | tf_op jit(solution)/shard_map/all_to_all | solution.py:15
  618.9 9.1 %copy-start.11 = (bf16[256,384]{1,0:T(8,128)(2,1)S(1)}, bf16[256,384]{1,0:T(8,128)(2,1)}, u32[]{:S(2)}) copy-start(bf16[256,384]{1,0:T(8,128)(2,1)} %copy-done.10) | copy-start | bytes 589828
  618.9 205.4 %copy-start.1 = (bf16[1,3072,384]{2,1,0:T(8,128)(2,1)S(1)}, bf16[1,3072,384]{2,1,0:T(8,128)(2,1)}, u32[]{:S(2)}) copy-start(bf16[1,3072,384]{2,1,0:T(8,128)(2,1)} %param.19) | copy-start | bytes 7077892
  626.7 16.0 %collective-permute-start.1 = (f32[128,384]{1,0:T(8,128)S(1)}, f32[128,384]{1,0:T(8,128)S(1)}, u32[]{:S(2)}, u32[]{:S(2)}) collective-permute-start(f32[128,384]{1,0:T(8,128)S(1)} %constant_dynamic-slice_fusion.6), channel_id=1, source_target_pairs={{0,64},{64,0},{1,65},{65,1},{2,66},{66,2},{3,67},{67,3},{4,68},{68... | collective-permute-start | bytes 589832 | tf_op jit(solution)/shard_map/ppermute | solution.py:57
Sparse Core Ops, SparseCore 0:
  50.4 61.7 all-gather.4
  193.3 47.9 all-gather.8
  275.6 54.0 all-gather.6
  376.9 127.8 reduce-scatter.5
  507.0 49.9 reduce-scatter.7
  559.8 109.6 reduce-scatter.13
  672.5 111.8 reduce-scatter.11
  787.3 37.0 reduce-scatter.9
where the time goes:
time: 833 us; the launch traced here: 831 us
  waiting for transfers between devices  542 us (65%)
  local copies, waits for them, and re-layouts  83.4 us (10%)
  matrix products  62.3 us (7%)
  blocking collectives  57.6 us (7%)
  starting transfers between devices  41.3 us (5%)
  other arithmetic  28 us (3%)
  between operations  15.1 us (2%)
    reduce_scatter x3, waiting for transfers between devices, sum_in_order(): pieces = lax.psum_scatter(pieces, axes[k], scatter_dimension=0, tiled=True)  168 us
    reduce_scatter x1, waiting for transfers between devices, on_device(): lax.psum_scatter(lax.dot_general(columns, attn, (((0,), (0,)), ((), ())),...  115 us
    all_to_all x3, waiting for transfers between devices, sum_at_owner(): lax.all_to_all(pieces, axis, split_axis=0, concat_axis=0, tiled=True)  105 us
    all_gather x1, waiting for transfers between devices, sent_together(): lax.all_gather(both, axis, axis=dim, tiled=True)  59.9 us
    all_to_all x4, waiting for transfers between devices, copy_for_each(): return lax.all_to_all(copies, axis, split_axis=0, concat_axis=0, tiled=True)  38.6 us
    all_gather x1, blocking collectives, on_device(): lax.all_gather(lse.T, ROW, axis=0, tiled=True)  29.6 us
    all_gather x1, blocking collectives, on_device(): lax.all_gather(dsum, ROW, axis=0, tiled=True)  28 us
    dynamic_slice x40, local copies, waits for them, and re-layouts, on_device(): carry, unused = lax.scan(attend, carry, blocks)  27.8 us
  transfers between devices with their start and end apart: 17, of which 14 were waited for; matrix products, arithmetic and copies ran while one was open for 10% of the time, Pallas kernels for 0%

commit v1 on v0

--- a/solution.py
+++ b/solution.py
@@ -8,6 +8,13 @@
 ROW = ("row_0", "row_1")
 GROUP_ROW = ("group", "row_0", "row_1")
 EPS = 1e-06
+
+
+def all_by_exchange(x, mesh_axis, d):
+    n_dev = lax.axis_size(mesh_axis)
+    blocks = jnp.stack([x for _ in range(n_dev)])
+    blocks = lax.all_to_all(blocks, mesh_axis, split_axis=0, concat_axis=0)
+    return jnp.concatenate(blocks, axis=d)
 
 
 def copy_for_each(array, axis):
@@ -212,7 +219,7 @@
             attn_grad.dtype
         ),
         lax.all_gather(lse.T, ROW, axis=0, tiled=True),
-        lax.all_gather(dsum, ROW, axis=0, tiled=True),
+        all_by_exchange(dsum, ROW, 0),
     )
     query_blocks = (
         gathered[0].reshape(block_count, tok, width),

time: 833 us -> 833 us (level)
  blocking collectives: 57.6 us -> 29.6 us
  waiting for transfers between devices: 542 us -> 565 us
    all_gather x1 -> x0, blocking collectives: 28 us -> none  [on_device(): lax.all_gather(dsum, ROW, axis=0, tiled=True)]
    all_gather x1, waiting for transfers between devices: 10.1 us -> 33.5 us  [on_device(): lax.all_gather(attn_grad.astype(jnp.float32), ROW, axis=0, tiled=True)]
  transfers between devices with their start and end apart: 17 -> 18, of which waited for: 14 -> 14; matrix products, arithmetic and copies ran while one was open for 10% -> 10% of each run, Pallas kernels for 0% -> 0%
where the time goes in v1:
time: 833 us; the launch traced here: 831 us
  waiting for transfers between devices  565 us (68%)
  local copies, waits for them, and re-layouts  84 us (10%)
  matrix products  62.3 us (7%)
  starting transfers between devices  45.2 us (5%)
  blocking collectives  29.6 us (4%)
  other arithmetic  28 us (3%)
  between operations  15.1 us (2%)
    reduce_scatter x3, waiting for transfers between devices, sum_in_order(): pieces = lax.psum_scatter(pieces, axes[k], scatter_dimension=0, tiled=True)  168 us
    reduce_scatter x1, waiting for transfers between devices, on_device(): lax.psum_scatter(lax.dot_general(columns, attn, (((0,), (0,)), ((), ())),...  114 us
    all_to_all x3, waiting for transfers between devices, sum_at_owner(): lax.all_to_all(pieces, axis, split_axis=0, concat_axis=0, tiled=True)  105 us
    all_gather x1, waiting for transfers between devices, sent_together(): lax.all_gather(both, axis, axis=dim, tiled=True)  59.9 us
    all_to_all x4, waiting for transfers between devices, copy_for_each(): return lax.all_to_all(copies, axis, split_axis=0, concat_axis=0, tiled=True)  38.6 us
    all_gather x1, waiting for transfers between devices, on_device(): lax.all_gather(attn_grad.astype(jnp.float32), ROW, axis=0, tiled=True)  33.5 us
    all_gather x1, blocking collectives, on_device(): lax.all_gather(lse.T, ROW, axis=0, tiled=True)  29.6 us
    dynamic_slice x40, local copies, waits for them, and re-layouts, on_device(): carry, unused = lax.scan(attend, carry, blocks)  27.7 us
  transfers between devices with their start and end apart: 18, of which 14 were waited for; matrix products, arithmetic and copies ran while one was open for 10% of the time, Pallas kernels for 0%

profile of v1, /device:TPU:1, one launch (start us, length us, event | category | flops | bytes accessed | tf_op | source)
XLA Modules:
  0.0 830.7 jit_solution(2184668806272117031)
XLA Ops:
  7.2 1.3 fusion.48
  8.6 1.3 broadcast_in_dim.24
  9.8 6.8 all-to-all-start
  18.1 19.2 %all-to-all-done = bf16[8,256,384]{2,1,0:T(8,128)(2,1)} async-done(((bf16[8,256,384]{2,1,0:T(8,128)(2,1)}), bf16[8,256,384]{2,1,0:T(8,128)(2,1)}, u32[]{:S(2)}, u32[]{:S(2)}) %all-to-all-start) | async-done | bytes 1572896 | tf_op jit(solution)/shard_map/all_to_all | solution.py:22
  37.3 2.6 copy.167
  39.9 1.9 convert_reduce_fusion
  43.4 5.3 fusion.37
  51.1 1.1 copy.171
  52.2 59.9 %all-gather.5.cloned.1.call-done = bf16[2048,768]{1,0:T(8,128)(2,1)} async-done(((bf16[256,768]{1,0:T(8,128)(2,1)}), bf16[2048,768]{1,0:T(8,128)(2,1)}) %all-gather.5.cloned.1.call-update) | async-done | bytes 3145744 | tf_op jit(solution)/shard_map/all_gather | solution.py:38
  112.1 3.9 fusion.59
  116.0 2.6 copy.172
  118.6 2.7 copy.170
  121.2 15.0 %while.39 = (s32[]{:T(128)}, f32[3,256]{1,0:T(4,128)S(1)}, f32[3,256]{1,0:T(4,128)S(1)}, f32[256,3,128]{0,2,1:T(8,128)S(1)}, bf16[8,256,384]{1,2,0:T(8,128)(2,1)...) while((s32[]{:T(128)}, f32[3,256]{1,0:T(4,128)S(1)}, ...), condition=%wide.region_6.7_spmd.clone, body=%wide.region_3.6_spmd.clone.sunk | while | flops 102142464 | bytes 4571253 | solution.py:159
  137.0 2.7 convolution_bitcast_fusion.2
  139.7 6.0 all-to-all-start.1
  145.8 37.4 %all-to-all-done.1 = f32[8,256,384]{2,1,0:T(8,128)} async-done(((f32[8,256,384]{2,1,0:T(8,128)}), f32[8,256,384]{2,1,0:T(8,128)}, u32[]{:S(2)}, u32[]{:S(2)}) %all-to-all-start.1) | async-done | bytes 3145760 | tf_op jit(solution)/shard_map/all_to_all | solution.py:53
  183.2 1.3 broadcast_in_dim.25
  184.5 5.1 all-to-all-start.3
  190.4 1.3 fusion.52
  191.7 2.1 reduce_sum.102
  193.7 16.6 %all-to-all-done.3 = bf16[8,256,384]{1,2,0:T(8,128)(2,1)} async-done(((bf16[8,256,384]{1,2,0:T(8,128)(2,1)}), bf16[8,256,384]{1,2,0:T(8,128)(2,1)}, u32[]{:S(2)}, u32[]{:S(2)}) %all-to-all-start.3) | async-done | bytes 1572896 | tf_op jit(solution)/shard_map/all_to_all | solution.py:22
  210.4 4.0 multiply_convert_fusion.2
  215.5 1.3 broadcast_in_dim.26
  216.7 5.1 all-to-all-start.4
  221.8 3.5 convert_element_type.155
  226.1 1.1 copy.189
  227.2 1.7 copy.184
  229.0 1.7 copy.187
  230.7 3.6 copy.210
  234.3 4.2 subtract_multiply_fusion
  238.5 1.7 copy.178
  240.3 29.6 %all_gather.14 = f32[2048,3]{0,1:T(4,128)} all-gather(f32[256,3]{0,1:T(4,128)S(1)} %bitcast.245), channel_id=1, replica_groups=mesh['group'=2,'row_0'=4,'row_1'=2,'head'=8] {'row_0','row_1'}, dimensions={0}, use_global_device_ids=true | all-gather | bytes 27648 | tf_op jit(solution)/shard_map/all_gather | solution.py:221
  269.9 3.3 convert_multiply_fusion
  273.2 1.2 copy.179
  274.4 1.1 copy.177
  276.1 4.0 all-to-all-start.5
  280.3 15.6 %while.40 = (s32[]{:T(128)}, f32[256,3,128]{0,2,1:T(8,128)S(1)}, bf16[8,256,384]{1,2,0:T(8,128)(2,1)}, bf16[256,3,128]{2,0,1:T(8,128)(2,1)S(1)}, f32[3,256]{1,0:...) while((s32[]{:T(128)}, f32[256,3,128]{0,2,1:T(8,128)S(1)}, ...), condition=%wide.region_11.12_spmd.clone, body=%wide.region_10.11_spmd.clone.sunk | while | flops 152174592 | bytes 4135035 | solution.py:212
  280.3 1.1 constant_dynamic-slice_fusion.13
  296.1 33.5 %all-gather.7.cloned.1.call-done = bf16[2048,384]{1,0:T(8,128)(2,1)} async-done(((bf16[256,384]{1,0:T(8,128)(2,1)}), bf16[2048,384]{1,0:T(8,128)(2,1)}) %all-gather.7.cloned.1.call-update) | async-done | bytes 1572880 | tf_op jit(solution)/shard_map/all_gather | solution.py:218
  329.6 25.8 %while.41 = (s32[]{:T(128)}, f32[256,3,128]{0,2,1:T(8,128)S(1)}, f32[256,3,128]{0,2,1:T(8,128)S(1)}, bf16[8,256,384]{2,1,0:T(8,128)(2,1)}, bf16[256,3,128]{2,0,1...) while((s32[]{:T(128)}, f32[256,3,128]{0,2,1:T(8,128)S(1)}, ...), condition=%wide.region_13.14_spmd.clone, body=%wide.region_12.13_spmd.clone.sunk | while | flops 202899456 | bytes 6703240 | solution.py:252
  355.9 9.3 %broadcast_multiply_fusion = f32[3072,3,384]{2,0,1:T(8,128)} fusion(f32[]{:T(128)S(6)} %convert_element_type.185, f32[256,3072]{1,0:T(8,128)} %subtract_multiply_fusion, f32[3072]{0:T(1024)S(1)} %bitcast.249, f32[3072]{0:T(1024)S(1)} %bitcast.248, bf16[1,256,384]{2,1,0:T(8,128)(2,1)S(1)} %copy.192, bf16[1,256,384]{2,1,0:T(8,128)(2,1)S(1)} %copy.191, ...), kind=kOutput, calls=%fused_computation.47 | convolution fusion | flops 1819607040 | bytes 17915908 | tf_op jit(solution)/shard_map/tc,pte->cpe/dot_general | solution.py:278
  365.2 11.7 %copy.197 = f32[4,2,2,192,3,384]{5,3,4,2,1,0:T(8,128)} copy(f32[4,2,2,192,3,384]{5,3,2,0,1,4:T(8,128)} %bitcast.214) | data formatting | bytes 28311552 | tf_op jit(solution)/shard_map/transpose | solution.py:84
  376.9 127.6 %reduce-scatter.6.cloned.1.call-done = f32[4,192,3,384]{3,1,2,0:T(8,128)} async-done(((f32[16,192,3,384]{3,1,2,0:T(8,128)}), f32[4,192,3,384]{3,1,2,0:T(8,128)}) %reduce-scatter.6.cloned.1.call-update) | async-done | bytes 3538960 | tf_op jit(solution)/shard_map/reduce_scatter | solution.py:87
  504.6 1.3 collective-permute-start
  505.9 4.5 collective-permute-done
  510.4 4.0 fusion.45
  515.4 5.0 convolution_multiply_fusion.3
  520.4 6.9 convolution_bitcast_fusion.3
  527.3 6.1 all-to-all-start.6
  534.5 1.8 copy.219
  536.3 34.7 %all-to-all-done.6 = f32[8,256,384]{2,1,0:T(8,128)} async-done(((f32[8,256,384]{2,1,0:T(8,128)}), f32[8,256,384]{2,1,0:T(8,128)}, u32[]{:S(2)}, u32[]{:S(2)}) %all-to-all-start.6) | async-done | bytes 3145760 | tf_op jit(solution)/shard_map/all_to_all | solution.py:53
  571.0 5.3 all-to-all-start.2
  577.7 2.1 reduce_sum.105
  579.8 1.2 multiply_reduce_fusion.2
  581.0 32.9 %all-to-all-done.2 = f32[8,256,384]{2,1,0:T(8,128)} async-done(((f32[8,256,384]{2,1,0:T(8,128)}), f32[8,256,384]{2,1,0:T(8,128)}, u32[]{:S(2)}, u32[]{:S(2)}) %all-to-all-start.2) | async-done | bytes 3145760 | tf_op jit(solution)/shard_map/all_to_all | solution.py:53
  614.5 4.2 all-to-all-start.7
  618.7 2.3 reduce_sum.103
  620.9 2.8 all-to-all-done.7
  625.1 1.3 multiply_add_fusion
  626.4 1.1 collective-permute-start.1
  628.3 14.0 %collective-permute-done.1 = f32[128,384]{1,0:T(8,128)S(1)} collective-permute-done((f32[128,384]{1,0:T(8,128)S(1)}, f32[128,384]{1,0:T(8,128)S(1)}, u32[]{:S(2)}, u32[]{:S(2)}) %collective-permute-start.1) | collective-permute-done | bytes 196640 | tf_op jit(solution)/shard_map/ppermute | solution.py:64
  643.1 27.0 %reduce-scatter.14.cloned.1.call-done = f32[192,384]{1,0:T(8,128)} async-done(((f32[3072,384]{1,0:T(8,128)}), f32[192,384]{1,0:T(8,128)}) %reduce-scatter.14.cloned.1.call-update) | async-done | bytes 294928 | tf_op jit(solution)/shard_map/reduce_scatter | solution.py:292
  670.1 113.8 %reduce-scatter.12.cloned.1.call-done = f32[192,384]{1,0:T(8,128)} async-done(((f32[3072,384]{1,0:T(8,128)}), f32[192,384]{1,0:T(8,128)}) %reduce-scatter.12.cloned.1.call-update) | async-done | bytes 294928 | tf_op jit(solution)/shard_map/reduce_scatter | solution.py:284
  783.9 39.9 %reduce-scatter.10.cloned.1.call-done = f32[1,192,3,384]{3,1,2,0:T(8,128)} async-done(((f32[2,192,3,384]{3,1,2,0:T(8,128)}), f32[1,192,3,384]{3,1,2,0:T(8,128)}) %reduce-scatter.10.cloned.1.call-update) | async-done | bytes 884752 | tf_op jit(solution)/shard_map/reduce_scatter | solution.py:87
  (229 shorter events, 71.1 us)
Async XLA Ops:
  7.2 129.2 %copy-start = (bf16[1,3072,384]{2,1,0:T(8,128)(2,1)S(1)}, bf16[1,3072,384]{2,1,0:T(8,128)(2,1)}, u32[]{:S(2)}) copy-start(bf16[1,3072,384]{2,1,0:T(8,128)(2,1)} %param.19) | copy-start | bytes 7077892
  8.5 8.8 %copy-start.10 = (f32[1,8,3,3072]{3,1,2,0:T(8,128)S(1)}, f32[1,8,3,3072]{3,1,2,0:T(8,128)}, u32[]{:S(2)}) copy-start(f32[1,8,3,3072]{3,1,2,0:T(8,128)} %param.17) | copy-start | bytes 884740
  9.8 27.5 %all-to-all-start = ((bf16[8,256,384]{2,1,0:T(8,128)(2,1)}), bf16[8,256,384]{2,1,0:T(8,128)(2,1)}, u32[]{:S(2)}, u32[]{:S(2)}) async-start(bf16[8,256,384]{2,1,0:T(8,128)(2,1)} %broadcast_in_dim.24), calls=%async_computation | async-start | bytes 3145728 | tf_op jit(solution)/shard_map/all_to_all | solution.py:22
  16.6 95.5 %all-gather.5.cloned.1.call-start = ((), (), s32[]{:S(2)}) async-start(), calls=%async_computation.13 | async-start | bytes 3538944 | tf_op jit(solution)/shard_map/all_gather | solution.py:38
  39.9 2.0 copy-start.2
  42.4 192.0 %copy-start.15 = (f32[256]{0:T(256)}, f32[256]{0:T(256)S(1)}, u32[]{:S(2)}) copy-start(f32[256]{0:T(256)S(1)} %add_rsqrt_fusion) | copy-start | bytes 3076
  49.4 66.6 %copy-start.8 = (bf16[1,256,384]{2,1,0:T(8,128)(2,1)}, bf16[1,256,384]{2,1,0:T(8,128)(2,1)S(1)}, u32[]{:S(2)}) copy-start(bf16[1,256,384]{2,1,0:T(8,128)(2,1)S(1)} %get-tuple-element.437) | copy-start | bytes 589828
  136.3 0.7 copy-start.5
  139.7 6.0 copy-start.11
  139.7 43.5 %all-to-all-start.1 = ((f32[8,256,384]{2,1,0:T(8,128)}), f32[8,256,384]{2,1,0:T(8,128)}, u32[]{:S(2)}, u32[]{:S(2)}) async-start(f32[8,256,384]{2,1,0:T(8,128)} %convolution_bitcast_fusion.2), calls=%async_computation.1 | async-start | bytes 6291456 | tf_op jit(solution)/shard_map/all_to_all | solution.py:53
  184.5 25.9 %all-to-all-start.3 = ((bf16[8,256,384]{1,2,0:T(8,128)(2,1)}), bf16[8,256,384]{1,2,0:T(8,128)(2,1)}, u32[]{:S(2)}, u32[]{:S(2)}) async-start(bf16[8,256,384]{1,2,0:T(8,128)(2,1)} %broadcast_in_dim.25), calls=%async_computation.3 | async-start | bytes 3145728 | tf_op jit(solution)/shard_map/all_to_all | solution.py:22
  189.6 106.5 %all-gather.9.cloned.1.call-start = ((), (), s32[]{:S(2)}) async-start(), calls=%async_computation.20 | async-start | bytes 1769472 | tf_op jit(solution)/shard_map/all_gather | solution.py:217
  216.7 53.2 %all-to-all-start.4 = ((bf16[8,256,384]{1,2,0:T(8,128)(2,1)}), bf16[8,256,384]{1,2,0:T(8,128)(2,1)}, u32[]{:S(2)}, u32[]{:S(2)}) async-start(bf16[8,256,384]{1,2,0:T(8,128)(2,1)} %broadcast_in_dim.26), calls=%async_computation.4 | async-start | bytes 3145728 | tf_op jit(solution)/shard_map/all_to_all | solution.py:22
  221.8 107.8 %all-gather.7.cloned.1.call-start = ((), (), s32[]{:S(2)}) async-start(), calls=%async_computation.14 | async-start | bytes 1769472 | tf_op jit(solution)/shard_map/all_gather | solution.py:218
  276.1 20.1 %all-to-all-start.5 = ((f32[8,256,3]{1,2,0:T(4,128)}), f32[8,256,3]{1,2,0:T(4,128)}, u32[]{:S(2)}, u32[]{:S(2)}) async-start(f32[8,256,3]{1,2,0:T(4,128)} %stack.4), calls=%async_computation.5 | async-start | bytes 65536 | tf_op jit(solution)/shard_map/all_to_all | solution.py:16
  280.0 224.4 %reduce-scatter.6.cloned.1.call-start = ((), (), s32[]{:S(2)}) async-start(), calls=%async_computation.15 | async-start | bytes 17694720 | tf_op jit(solution)/shard_map/reduce_scatter | solution.py:87
  280.2 49.4 %copy-start.3 = (f32[256,3,128]{0,2,1:T(8,128)S(1)}, f32[256,3,128]{0,2,1:T(8,128)}, u32[]{:S(2)}) copy-start(f32[256,3,128]{0,2,1:T(8,128)} %custom-call.5) | copy-start | bytes 1179652
  280.3 49.4 %copy-start.4 = (bf16[256,3,128]{2,0,1:T(8,128)(2,1)S(1)}, bf16[256,3,128]{2,0,1:T(8,128)(2,1)}, u32[]{:S(2)}) copy-start(bf16[256,3,128]{2,0,1:T(8,128)(2,1)} %copy.187) | copy-start | bytes 589828
  329.6 26.2 %copy-start.12 = (f32[1,3072]{1,0:T(1,128)S(1)}, f32[1,3072]{1,0:T(1,128)}, u32[]{:S(2)}) copy-start(f32[1,3072]{1,0:T(1,128)} %get-tuple-element.440) | copy-start | bytes 36868
  329.6 26.2 %copy-start.13 = (f32[1,3072]{1,0:T(1,128)S(1)}, f32[1,3072]{1,0:T(1,128)}, u32[]{:S(2)}) copy-start(f32[1,3072]{1,0:T(1,128)} %get-tuple-element.441) | copy-start | bytes 36868
  376.8 127.7 %copy-start.9 = (bf16[256,384]{1,0:T(8,128)(2,1)S(1)}, bf16[256,384]{1,0:T(8,128)(2,1)}, u32[]{:S(2)}) copy-start(bf16[256,384]{1,0:T(8,128)(2,1)} %get-tuple-element.447) | copy-start | bytes 589828
  376.9 199.4 %reduce-scatter.8.cloned.1.call-start = ((), (), s32[]{:S(2)}) async-start(), calls=%async_computation.16 | async-start | bytes 5308416 | tf_op jit(solution)/shard_map/reduce_scatter | solution.py:87
  504.5 165.6 %reduce-scatter.14.cloned.1.call-start = ((), (), s32[]{:S(2)}) async-start(), calls=%async_computation.19 | async-start | bytes 5013504 | tf_op jit(solution)/shard_map/reduce_scatter | solution.py:292
  504.6 5.8 collective-permute-start
  514.4 1.0 copy-start.6
  514.5 269.5 %reduce-scatter.12.cloned.1.call-start = ((), (), s32[]{:S(2)}) async-start(), calls=%async_computation.18 | async-start | bytes 5013504 | tf_op jit(solution)/shard_map/reduce_scatter | solution.py:284
  527.3 6.1 copy-start.7
  527.3 43.7 %all-to-all-start.6 = ((f32[8,256,384]{2,1,0:T(8,128)}), f32[8,256,384]{2,1,0:T(8,128)}, u32[]{:S(2)}, u32[]{:S(2)}) async-start(f32[8,256,384]{2,1,0:T(8,128)} %convolution_bitcast_fusion.3), calls=%async_computation.6 | async-start | bytes 6291456 | tf_op jit(solution)/shard_map/all_to_all | solution.py:53
  571.0 42.9 %all-to-all-start.2 = ((f32[8,256,384]{2,1,0:T(8,128)}), f32[8,256,384]{2,1,0:T(8,128)}, u32[]{:S(2)}, u32[]{:S(2)}) async-start(f32[8,256,384]{2,1,0:T(8,128)} %bitcast.226), calls=%async_computation.2 | async-start | bytes 6291456 | tf_op jit(solution)/shard_map/all_to_all | solution.py:53
  576.3 247.6 %reduce-scatter.10.cloned.1.call-start = ((), (), s32[]{:S(2)}) async-start(), calls=%async_computation.17 | async-start | bytes 2654208 | tf_op jit(solution)/shard_map/reduce_scatter | solution.py:87
  577.7 41.0 %copy-start.14 = (f32[384]{0:T(512)}, f32[384]{0:T(512)S(1)}, u32[]{:S(2)}) copy-start(f32[384]{0:T(512)S(1)} %fusion.54) | copy-start | bytes 4612
  614.5 9.3 %all-to-all-start.7 = ((f32[8,1,512]{2,1,0:T(1,128)}), f32[8,1,512]{2,1,0:T(1,128)S(1)}, u32[]{:S(2)}, u32[]{:S(2)}) async-start(f32[8,1,512]{2,1,0:T(1,128)} %broadcast_in_dim.27), calls=%async_computation.7 | async-start | bytes 32768 | tf_op jit(solution)/shard_map/all_to_all | solution.py:22
  618.7 205.2 %copy-start.1 = (bf16[1,3072,384]{2,1,0:T(8,128)(2,1)S(1)}, bf16[1,3072,384]{2,1,0:T(8,128)(2,1)}, u32[]{:S(2)}) copy-start(bf16[1,3072,384]{2,1,0:T(8,128)(2,1)} %param.19) | copy-start | bytes 7077892
  626.4 15.9 %collective-permute-start.1 = (f32[128,384]{1,0:T(8,128)S(1)}, f32[128,384]{1,0:T(8,128)S(1)}, u32[]{:S(2)}, u32[]{:S(2)}) collective-permute-start(f32[128,384]{1,0:T(8,128)S(1)} %constant_dynamic-slice_fusion.6), channel_id=1, source_target_pairs={{0,64},{64,0},{1,65},{65,1},{2,66},{66,2},{3,67},{67,3},{4,68},{68... | collective-permute-start | bytes 589832 | tf_op jit(solution)/shard_map/ppermute | solution.py:64
Sparse Core Ops, SparseCore 0:
  50.4 61.7 all-gather.4
  193.3 47.9 all-gather.8
  275.6 53.9 all-gather.6
  377.0 127.4 reduce-scatter.5
  506.7 49.9 reduce-scatter.7
  559.5 110.5 reduce-scatter.13
  673.1 110.7 reduce-scatter.11
  786.9 36.9 reduce-scatter.9
